TPU v7x, 256 devices: a whole 4x4x8 slice. The times are simulated.
256 devices in a mesh: rows: 16 (over z, core), samp: 16 (over y, x).
Axes of the slice: x: 4, y: 4, z: 8, core: 2. Of those that a mesh axis runs over, the one named last changes fastest.
Arguments:
- right_sides: float32 [576, 128, 2048], P('rows', None, 'samp'), may hold values from -6 to 6
- factor_blocks: float32 [576, 6, 128, 128], P('rows', None, 'samp'), may hold values from -0.21875 to 0.21875
- block_columns: int32 [576, 6], P('rows'), may hold values from 0 to 8, as said below
- pivot_rows: int32 [8], replicated, may hold values from 0 to 575, as said below
- diag_inverse: float32 [8, 128, 128], replicated
Outputs:
- solved_blocks: float32 [8, 128, 2048], P(None, None, 'samp')
- updated_sides: float32 [576, 128, 2048], P('rows', None, 'samp')
Inputs may be any that keep to these rules, and one draw needn't show every extreme that they name: `block_columns`: in each block row the values below 8 are distinct; 8 marks an empty slot. `pivot_rows`: the 8 positions are distinct.
All inputs are finite; a program needn't handle non-finite values.
Results may differ from a plain program's by a relative error of at most 0.0001.
Values sent between devices are 32-bit elements; how exact they have to be, the bound alone decides.
No kernel may reach another device: no remote copies, remote signals or barrier semaphores. Data moves between devices by JAX's collectives and lax.ppermute only.
A program may use at most 128 MiB of HBM per device.

v0:
```python
import jax
import jax.numpy as jnp
from jax import lax
from jax.sharding import PartitionSpec as P


def spread(block, axis, source):
    block = jnp.where(lax.axis_index(axis) == source, block, jnp.zeros_like(block))
    return lax.psum(block, axis)


def local(right_sides, factor_blocks, block_columns, pivot_rows, diag_inverse):
    highest = lax.Precision.HIGHEST
    row_count = right_sides.shape[0]
    step_count = pivot_rows.shape[0]
    local_ids = lax.axis_index("rows") * row_count + jnp.arange(row_count, dtype=jnp.int32)
    matches = local_ids[:, None] == pivot_rows[None, :]
    targets = jnp.arange(step_count, dtype=jnp.int32)
    row_rank = step_count + jnp.sum(jnp.where(matches, targets[None, :] - step_count, 0), axis=1)
    selector = (
        (block_columns[:, :, None] == targets[None, None, :])
        & (targets[None, None, :] < row_rank[:, None, None])
    ).astype(jnp.float32)
    current = right_sides
    solved = []
    for column in range(step_count):
        owner_index = pivot_rows[column] // row_count
        slot_index = pivot_rows[column] % row_count
        pivot_side = lax.dynamic_index_in_dim(current, slot_index, 0, keepdims=False)
        candidate = jnp.dot(diag_inverse[column], pivot_side, precision=highest)
        solved_now = spread(candidate, "rows", owner_index)
        column_part = jnp.einsum(
            "rs,rsab->rab", selector[:, :, column], factor_blocks, precision=highest
        )

        def apply_block(piece, start, solved_now=solved_now):
            return jnp.einsum("rab,bn->ran", piece, solved_now, precision=highest)

        correction = apply_block(
            lax.all_gather(column_part, "samp", axis=1, tiled=True), jnp.int32(0)
        )
        current = current - correction
        solved.append(solved_now)
    return (jnp.stack(solved), current)


def solution(mesh):
    placed = (P("rows", None, "samp"), P("rows", None, "samp", None), P("rows", None), P(), P())
    return jax.shard_map(
        local,
        mesh=mesh,
        in_specs=placed,
        out_specs=(P(None, None, "samp"), P("rows", None, "samp")),
        check_vma=False,
    )
```

profile of v0, /device:TPU:1, one launch (start us, length us, event | category | flops | bytes accessed | tf_op | source)
XLA Modules:
  0.0 864.1 jit_solution(17479028503229165503)
XLA Ops:
  8.1 1.6 fusion.73
  11.7 1.8 fusion.23
  13.6 0.7 select_reduce_fusion
  14.3 0.7 fusion.64
  15.2 1.5 fusion.14
  16.9 1.5 fusion.12
  20.5 97.0 %all-reduce.9.cloned.1.call-done = f32[128,128]{0,1:T(8,128)} async-done(((f32[128,128]{0,1:T(8,128)}), f32[128,128]{0,1:T(8,128)}) %all-reduce.9.cloned.1.call-update) | async-done | bytes 65552 | tf_op jit(solution)/shard_map/psum | solution.py:9
  117.5 3.9 convolution_subtract_fusion.7
  121.4 1.4 copy-done.2
  122.8 1.7 fusion.22
  124.6 1.5 fusion.10
  128.0 0.8 all-gather.11.cloned.1.call-done
  128.8 93.2 %all-reduce.11.cloned.1.call-done = f32[128,128]{0,1:T(8,128)} async-done(((f32[128,128]{0,1:T(8,128)}), f32[128,128]{0,1:T(8,128)}) %all-reduce.11.cloned.1.call-update) | async-done | bytes 65552 | tf_op jit(solution)/shard_map/psum | solution.py:9
  222.0 4.4 convolution_subtract_fusion.6
  226.5 1.8 fusion.21
  228.3 1.5 fusion.8
  231.9 94.0 %all-reduce.13.cloned.1.call-done = f32[128,128]{0,1:T(8,128)} async-done(((f32[128,128]{0,1:T(8,128)}), f32[128,128]{0,1:T(8,128)}) %all-reduce.13.cloned.1.call-update) | async-done | bytes 65552 | tf_op jit(solution)/shard_map/psum | solution.py:9
  325.8 3.9 convolution_subtract_fusion.5
  329.7 1.4 copy-done.1
  331.1 1.7 fusion.20
  333.1 1.5 fusion.6
  336.6 94.2 %all-reduce.15.cloned.1.call-done = f32[128,128]{0,1:T(8,128)} async-done(((f32[128,128]{0,1:T(8,128)}), f32[128,128]{0,1:T(8,128)}) %all-reduce.15.cloned.1.call-update) | async-done | bytes 65552 | tf_op jit(solution)/shard_map/psum | solution.py:9
  430.8 4.4 convolution_subtract_fusion.4
  435.2 1.8 fusion.19
  437.0 1.5 fusion.4
  440.8 93.8 %all-reduce.17.cloned.1.call-done = f32[128,128]{0,1:T(8,128)} async-done(((f32[128,128]{0,1:T(8,128)}), f32[128,128]{0,1:T(8,128)}) %all-reduce.17.cloned.1.call-update) | async-done | bytes 65552 | tf_op jit(solution)/shard_map/psum | solution.py:9
  534.6 3.9 convolution_subtract_fusion.3
  538.5 1.4 copy-done.3
  539.9 1.7 fusion.18
  541.7 1.5 fusion.2
  545.0 94.6 %all-reduce.19.cloned.1.call-done = f32[128,128]{0,1:T(8,128)} async-done(((f32[128,128]{0,1:T(8,128)}), f32[128,128]{0,1:T(8,128)}) %all-reduce.19.cloned.1.call-update) | async-done | bytes 65552 | tf_op jit(solution)/shard_map/psum | solution.py:9
  639.6 4.4 convolution_subtract_fusion.2
  644.0 1.8 fusion.17
  648.4 95.0 %all-reduce.21.cloned.1.call-done = f32[128,128]{0,1:T(8,128)} async-done(((f32[128,128]{0,1:T(8,128)}), f32[128,128]{0,1:T(8,128)}) %all-reduce.21.cloned.1.call-update) | async-done | bytes 65552 | tf_op jit(solution)/shard_map/psum | solution.py:9
  743.4 3.9 convolution_subtract_fusion.1
  747.3 1.4 copy-done.4
  748.7 1.8 fusion.16
  750.5 1.5 fusion
  752.7 0.6 bitcast_dynamic-update-slice_fusion.6
  753.3 0.6 bitcast_dynamic-update-slice_fusion.5
  753.9 0.6 bitcast_dynamic-update-slice_fusion.4
  754.6 1.5 bitcast_dynamic-update-slice_fusion.3
  756.0 1.5 bitcast_dynamic-update-slice_fusion.2
  757.5 1.5 bitcast_dynamic-update-slice_fusion.1
  759.0 89.1 %all-reduce.23.cloned.1.call-done = f32[128,128]{0,1:T(8,128)} async-done(((f32[128,128]{0,1:T(8,128)}), f32[128,128]{0,1:T(8,128)}) %all-reduce.23.cloned.1.call-update) | async-done | bytes 65552 | tf_op jit(solution)/shard_map/psum | solution.py:9
  848.1 1.5 bitcast_dynamic-update-slice_fusion
  849.5 2.0 copy.34
  851.6 5.1 convolution_subtract_fusion
  (71 shorter events, 3.3 us)
Async XLA Ops:
  8.0 7.2 copy-start
  8.0 109.5 %copy-start.6 = (f32[36,128,128]{2,1,0:T(8,128)S(1)}, f32[36,128,128]{2,1,0:T(8,128)}, u32[]{:S(2)}) copy-start(f32[36,128,128]{2,1,0:T(8,128)} %param.5) | copy-start | bytes 7077892
  8.0 109.5 %all-reduce.9.cloned.1.call-start = ((), (), s32[]{:S(2)}) async-start(), calls=%async_computation | async-start | bytes 131072 | tf_op jit(solution)/shard_map/psum | solution.py:9
  13.5 104.0 %all-gather.9.cloned.1.call-start = ((), (), s32[]{:S(2)}) async-start(), calls=%async_computation.1 | async-start | bytes 2506752 | tf_op jit(solution)/shard_map/all_gather | solution.py:40
  16.7 112.2 %all-gather.11.cloned.1.call-start = ((), (), s32[]{:S(2)}) async-start(), calls=%async_computation.3 | async-start | bytes 2506752 | tf_op jit(solution)/shard_map/all_gather | solution.py:40
  18.4 203.7 %all-reduce.11.cloned.1.call-start = ((), (), s32[]{:S(2)}) async-start(), calls=%async_computation.2 | async-start | bytes 131072 | tf_op jit(solution)/shard_map/psum | solution.py:9
  121.4 1.4 copy-start.2
  124.6 107.3 %all-gather.13.cloned.1.call-start = ((), (), s32[]{:S(2)}) async-start(), calls=%async_computation.5 | async-start | bytes 2506752 | tf_op jit(solution)/shard_map/all_gather | solution.py:40
  126.1 199.7 %all-reduce.13.cloned.1.call-start = ((), (), s32[]{:S(2)}) async-start(), calls=%async_computation.4 | async-start | bytes 131072 | tf_op jit(solution)/shard_map/psum | solution.py:9
  228.2 108.3 %all-gather.15.cloned.1.call-start = ((), (), s32[]{:S(2)}) async-start(), calls=%async_computation.7 | async-start | bytes 2506752 | tf_op jit(solution)/shard_map/all_gather | solution.py:40
  229.8 201.0 %all-reduce.15.cloned.1.call-start = ((), (), s32[]{:S(2)}) async-start(), calls=%async_computation.6 | async-start | bytes 131072 | tf_op jit(solution)/shard_map/psum | solution.py:9
  329.7 1.4 copy-start.1
  332.9 107.9 %all-gather.17.cloned.1.call-start = ((), (), s32[]{:S(2)}) async-start(), calls=%async_computation.9 | async-start | bytes 2506752 | tf_op jit(solution)/shard_map/all_gather | solution.py:40
  334.6 200.0 %all-reduce.17.cloned.1.call-start = ((), (), s32[]{:S(2)}) async-start(), calls=%async_computation.8 | async-start | bytes 131072 | tf_op jit(solution)/shard_map/psum | solution.py:9
  437.0 108.0 %all-gather.19.cloned.1.call-start = ((), (), s32[]{:S(2)}) async-start(), calls=%async_computation.11 | async-start | bytes 2506752 | tf_op jit(solution)/shard_map/all_gather | solution.py:40
  438.5 201.1 %all-reduce.19.cloned.1.call-start = ((), (), s32[]{:S(2)}) async-start(), calls=%async_computation.10 | async-start | bytes 131072 | tf_op jit(solution)/shard_map/psum | solution.py:9
  538.5 1.4 copy-start.3
  541.7 106.7 %all-gather.21.cloned.1.call-start = ((), (), s32[]{:S(2)}) async-start(), calls=%async_computation.13 | async-start | bytes 2506752 | tf_op jit(solution)/shard_map/all_gather | solution.py:40
  543.2 200.2 %all-reduce.21.cloned.1.call-start = ((), (), s32[]{:S(2)}) async-start(), calls=%async_computation.12 | async-start | bytes 131072 | tf_op jit(solution)/shard_map/psum | solution.py:9
  645.8 202.2 %all-reduce.23.cloned.1.call-start = ((), (), s32[]{:S(2)}) async-start(), calls=%async_computation.14 | async-start | bytes 131072 | tf_op jit(solution)/shard_map/psum | solution.py:9
  648.3 103.7 %copy-start.7 = (f32[128,128]{0,1:T(8,128)S(1)}, f32[128,128]{0,1:T(8,128)}, u32[]{:S(2)}) copy-start(f32[128,128]{0,1:T(8,128)} %all-reduce.9.cloned.1.call-done) | copy-start | bytes 196612
  648.3 104.3 %copy-start.8 = (f32[128,128]{0,1:T(8,128)S(1)}, f32[128,128]{0,1:T(8,128)}, u32[]{:S(2)}) copy-start(f32[128,128]{0,1:T(8,128)} %all-reduce.11.cloned.1.call-done) | copy-start | bytes 196612
  648.3 105.0 %copy-start.9 = (f32[128,128]{0,1:T(8,128)S(1)}, f32[128,128]{0,1:T(8,128)}, u32[]{:S(2)}) copy-start(f32[128,128]{0,1:T(8,128)} %all-reduce.13.cloned.1.call-done) | copy-start | bytes 196612
  648.4 105.6 %copy-start.10 = (f32[128,128]{0,1:T(8,128)S(1)}, f32[128,128]{0,1:T(8,128)}, u32[]{:S(2)}) copy-start(f32[128,128]{0,1:T(8,128)} %all-reduce.15.cloned.1.call-done) | copy-start | bytes 196612
  747.3 1.4 copy-start.4
  750.4 101.1 %copy-start.5 = (f32[36,128,128]{2,1,0:T(8,128)S(1)}, f32[36,128,128]{2,1,0:T(8,128)}, u32[]{:S(2)}) copy-start(f32[36,128,128]{2,1,0:T(8,128)} %copy-done.4) | copy-start | bytes 7077892
  750.5 101.1 %all-gather.23.cloned.1.call-start = ((), (), s32[]{:S(2)}) async-start(), calls=%async_computation.15 | async-start | bytes 2506752 | tf_op jit(solution)/shard_map/all_gather | solution.py:40
Sparse Core Ops, SparseCore 0:
  13.6 103.8 all-reduce.8
  124.7 97.2 all-reduce.10
  228.4 97.4 all-reduce.12
  333.0 97.7 all-reduce.14
  437.1 97.4 all-reduce.16
  541.8 97.7 all-reduce.18
  645.9 97.4 all-reduce.20
  750.6 97.4 all-reduce.22
Sparse Core Ops, SparseCore 1:
  17.2 56.2 all-gather.8
  75.8 53.0 all-gather.10
  132.0 52.8 all-gather.12
  231.4 50.5 all-gather.14
  337.0 50.5 all-gather.16
  440.2 50.5 all-gather.18
  545.4 50.5 all-gather.20
  753.4 50.5 all-gather.22
where the time goes:
time: 865 us; the launch traced here: 864 us
  waiting for transfers between devices  752 us (87%)
  matrix products  59.6 us (7%)
  between operations  31.1 us (4%)
  local copies, waits for them, and re-layouts  18.8 us (2%)
    psum x8, waiting for transfers between devices, spread(): return lax.psum(block, axis)  751 us
    dot_general x8, matrix products, apply_block(): return jnp.einsum('rab,bn->ran', piece, solved_now, precision=highest)  33.8 us
  transfers between devices with their start and end apart: 16, of which 9 were waited for; matrix products, arithmetic and copies ran while one was open for 7% of the time, Pallas kernels for 0%

commit v1 on v0

--- a/solution.py
+++ b/solution.py
@@ -6,7 +6,7 @@
 
 def spread(block, axis, source):
     block = jnp.where(lax.axis_index(axis) == source, block, jnp.zeros_like(block))
-    return lax.psum(block, axis)
+    return jnp.sum(lax.all_gather(block, axis), axis=0)
 
 
 def local(right_sides, factor_blocks, block_columns, pivot_rows, diag_inverse):

time: 865 us -> 821 us (0.949)
  waiting for transfers between devices: 752 us -> 695 us
  local copies, waits for them, and re-layouts: 18.8 us -> 30.7 us
    psum x8 -> x0, waiting for transfers between devices: 751 us -> none  [spread(): return lax.psum(block, axis)]
    all_gather x8, waiting for transfers between devices: 0.96 us -> 419 us  [local(): lax.all_gather(column_part, 'samp', axis=1, tiled=True)]
    all_gather x0 -> x8, waiting for transfers between devices: none -> 275 us  [spread(): return jnp.sum(lax.all_gather(block, axis), axis=0)]
    unnamed x30 -> x36, local copies, waits for them, and re-layouts: 14.6 us -> 27.4 us
  transfers between devices with their start and end apart: 16 -> 16, of which waited for: 9 -> 16; matrix products, arithmetic and copies ran while one was open for 7% -> 5% of each run, Pallas kernels for 0% -> 0%
where the time goes in v1:
time: 821 us; the launch traced here: 820 us
  waiting for transfers between devices  695 us (85%)
  matrix products  59 us (7%)
  local copies, waits for them, and re-layouts  30.7 us (4%)
  between operations  29.7 us (4%)
    all_gather x8, waiting for transfers between devices, local(): lax.all_gather(column_part, 'samp', axis=1, tiled=True)  419 us
    all_gather x8, waiting for transfers between devices, spread(): return jnp.sum(lax.all_gather(block, axis), axis=0)  275 us
    dot_general x8, matrix products, apply_block(): return jnp.einsum('rab,bn->ran', piece, solved_now, precision=highest)  33.2 us
    unnamed x36, local copies, waits for them, and re-layouts  27.4 us
  transfers between devices with their start and end apart: 16, of which 16 were waited for; matrix products, arithmetic and copies ran while one was open for 5% of the time, Pallas kernels for 0%

profile of v1, /device:TPU:1, one launch (start us, length us, event | category | flops | bytes accessed | tf_op | source)
XLA Modules:
  0.0 819.5 jit_solution(9201285238681898394)
XLA Ops:
  7.2 1.6 fusion.73
  10.8 1.8 fusion.23
  14.3 1.5 fusion.14
  17.8 36.8 %all-gather.41.cloned.1.call-done = f32[2048,128]{0,1:T(8,128)} async-done(((f32[128,128]{0,1:T(8,128)}), f32[2048,128]{0,1:T(8,128)}) %all-gather.41.cloned.1.call-update) | async-done | bytes 1048592 | tf_op jit(solution)/shard_map/all_gather | solution.py:9
  56.2 53.1 %all-gather.25.cloned.1.call-done = f32[36,128,128]{2,1,0:T(8,128)} async-done(((f32[36,8,128]{2,1,0:T(8,128)}), f32[36,128,128]{2,1,0:T(8,128)}) %all-gather.25.cloned.1.call-update) | async-done | bytes 2359312 | tf_op jit(solution)/shard_map/all_gather | solution.py:40
  109.3 3.9 convolution_subtract_fusion.7
  114.6 1.7 fusion.22
  116.6 1.5 fusion.12
  120.2 34.7 %all-gather.43.cloned.1.call-done = f32[2048,128]{0,1:T(8,128)} async-done(((f32[128,128]{0,1:T(8,128)}), f32[2048,128]{0,1:T(8,128)}) %all-gather.43.cloned.1.call-update) | async-done | bytes 1048592 | tf_op jit(solution)/shard_map/all_gather | solution.py:9
  154.9 1.4 copy.60
  156.5 53.0 %all-gather.27.cloned.1.call-done = f32[36,128,128]{2,1,0:T(8,128)} async-done(((f32[36,8,128]{2,1,0:T(8,128)}), f32[36,128,128]{2,1,0:T(8,128)}) %all-gather.27.cloned.1.call-update) | async-done | bytes 2359312 | tf_op jit(solution)/shard_map/all_gather | solution.py:40
  209.4 4.4 convolution_subtract_fusion.6
  213.8 1.8 fusion.21
  215.8 1.5 fusion.10
  219.0 35.1 %all-gather.45.cloned.1.call-done = f32[2048,128]{0,1:T(8,128)} async-done(((f32[128,128]{0,1:T(8,128)}), f32[2048,128]{0,1:T(8,128)}) %all-gather.45.cloned.1.call-update) | async-done | bytes 1048592 | tf_op jit(solution)/shard_map/all_gather | solution.py:9
  255.7 53.0 %all-gather.29.cloned.1.call-done = f32[36,128,128]{2,1,0:T(8,128)} async-done(((f32[36,8,128]{2,1,0:T(8,128)}), f32[36,128,128]{2,1,0:T(8,128)}) %all-gather.29.cloned.1.call-update) | async-done | bytes 2359312 | tf_op jit(solution)/shard_map/all_gather | solution.py:40
  308.7 3.9 convolution_subtract_fusion.5
  313.9 1.7 fusion.20
  316.1 1.5 fusion.8
  319.6 34.7 %all-gather.47.cloned.1.call-done = f32[2048,128]{0,1:T(8,128)} async-done(((f32[128,128]{0,1:T(8,128)}), f32[2048,128]{0,1:T(8,128)}) %all-gather.47.cloned.1.call-update) | async-done | bytes 1048592 | tf_op jit(solution)/shard_map/all_gather | solution.py:9
  354.2 1.4 copy.62
  355.8 53.1 %all-gather.31.cloned.1.call-done = f32[36,128,128]{2,1,0:T(8,128)} async-done(((f32[36,8,128]{2,1,0:T(8,128)}), f32[36,128,128]{2,1,0:T(8,128)}) %all-gather.31.cloned.1.call-update) | async-done | bytes 2359312 | tf_op jit(solution)/shard_map/all_gather | solution.py:40
  408.9 3.9 convolution_subtract_fusion.4
  414.2 1.7 fusion.19
  416.1 1.5 fusion.6
  419.6 34.9 %all-gather.49.cloned.1.call-done = f32[2048,128]{0,1:T(8,128)} async-done(((f32[128,128]{0,1:T(8,128)}), f32[2048,128]{0,1:T(8,128)}) %all-gather.49.cloned.1.call-update) | async-done | bytes 1048592 | tf_op jit(solution)/shard_map/all_gather | solution.py:9
  456.7 52.3 %all-gather.33.cloned.1.call-done = f32[36,128,128]{2,1,0:T(8,128)} async-done(((f32[36,8,128]{2,1,0:T(8,128)}), f32[36,128,128]{2,1,0:T(8,128)}) %all-gather.33.cloned.1.call-update) | async-done | bytes 2359312 | tf_op jit(solution)/shard_map/all_gather | solution.py:40
  509.0 3.9 convolution_subtract_fusion.3
  514.3 1.7 fusion.18
  516.2 1.5 fusion.4
  519.7 34.9 %all-gather.51.cloned.1.call-done = f32[2048,128]{0,1:T(8,128)} async-done(((f32[128,128]{0,1:T(8,128)}), f32[2048,128]{0,1:T(8,128)}) %all-gather.51.cloned.1.call-update) | async-done | bytes 1048592 | tf_op jit(solution)/shard_map/all_gather | solution.py:9
  554.6 1.4 copy.64
  556.8 52.3 %all-gather.35.cloned.1.call-done = f32[36,128,128]{2,1,0:T(8,128)} async-done(((f32[36,8,128]{2,1,0:T(8,128)}), f32[36,128,128]{2,1,0:T(8,128)}) %all-gather.35.cloned.1.call-update) | async-done | bytes 2359312 | tf_op jit(solution)/shard_map/all_gather | solution.py:40
  609.1 4.4 convolution_subtract_fusion.2
  613.5 1.8 fusion.17
  615.7 1.5 fusion.2
  619.3 34.5 %all-gather.53.cloned.1.call-done = f32[2048,128]{0,1:T(8,128)} async-done(((f32[128,128]{0,1:T(8,128)}), f32[2048,128]{0,1:T(8,128)}) %all-gather.53.cloned.1.call-update) | async-done | bytes 1048592 | tf_op jit(solution)/shard_map/all_gather | solution.py:9
  656.0 52.4 %all-gather.37.cloned.1.call-done = f32[36,128,128]{2,1,0:T(8,128)} async-done(((f32[36,8,128]{2,1,0:T(8,128)}), f32[36,128,128]{2,1,0:T(8,128)}) %all-gather.37.cloned.1.call-update) | async-done | bytes 2359312 | tf_op jit(solution)/shard_map/all_gather | solution.py:40
  708.4 3.9 convolution_subtract_fusion.1
  713.7 1.8 fusion.16
  715.6 1.5 fusion
  719.6 1.5 bitcast_dynamic-update-slice_fusion.3
  721.1 1.6 bitcast_dynamic-update-slice_fusion.2
  722.7 1.5 bitcast_dynamic-update-slice_fusion.1
  724.2 29.8 %all-gather.55.cloned.1.call-done = f32[2048,128]{0,1:T(8,128)} async-done(((f32[128,128]{0,1:T(8,128)}), f32[2048,128]{0,1:T(8,128)}) %all-gather.55.cloned.1.call-update) | async-done | bytes 1048592 | tf_op jit(solution)/shard_map/all_gather | solution.py:9
  756.2 2.0 copy.25
  758.2 49.7 %all-gather.39.cloned.1.call-done = f32[36,128,128]{2,1,0:T(8,128)} async-done(((f32[36,8,128]{2,1,0:T(8,128)}), f32[36,128,128]{2,1,0:T(8,128)}) %all-gather.39.cloned.1.call-update) | async-done | bytes 2359312 | tf_op jit(solution)/shard_map/all_gather | solution.py:40
  807.9 5.1 convolution_subtract_fusion
  (85 shorter events, 24.2 us)
Async XLA Ops:
  7.2 7.2 copy-start
  7.2 47.5 %all-gather.41.cloned.1.call-start = ((), (), s32[]{:S(2)}) async-start(), calls=%async_computation.8 | async-start | bytes 1114112 | tf_op jit(solution)/shard_map/all_gather | solution.py:9
  12.6 96.7 %all-gather.25.cloned.1.call-start = ((), (), s32[]{:S(2)}) async-start(), calls=%async_computation | async-start | bytes 2506752 | tf_op jit(solution)/shard_map/all_gather | solution.py:40
  14.3 95.0 %copy-start.9 = (f32[36,128,128]{2,1,0:T(8,128)S(1)}, f32[36,128,128]{2,1,0:T(8,128)}, u32[]{:S(2)}) copy-start(f32[36,128,128]{2,1,0:T(8,128)} %param.5) | copy-start | bytes 7077892
  15.8 139.1 %all-gather.43.cloned.1.call-start = ((), (), s32[]{:S(2)}) async-start(), calls=%async_computation.9 | async-start | bytes 1114112 | tf_op jit(solution)/shard_map/all_gather | solution.py:9
  113.2 1.4 copy-start.6
  116.4 93.1 %all-gather.27.cloned.1.call-start = ((), (), s32[]{:S(2)}) async-start(), calls=%async_computation.1 | async-start | bytes 2506752 | tf_op jit(solution)/shard_map/all_gather | solution.py:40
  118.1 136.1 %all-gather.45.cloned.1.call-start = ((), (), s32[]{:S(2)}) async-start(), calls=%async_computation.10 | async-start | bytes 1114112 | tf_op jit(solution)/shard_map/all_gather | solution.py:9
  215.6 93.1 %all-gather.29.cloned.1.call-start = ((), (), s32[]{:S(2)}) async-start(), calls=%async_computation.2 | async-start | bytes 2506752 | tf_op jit(solution)/shard_map/all_gather | solution.py:40
  217.3 136.9 %all-gather.47.cloned.1.call-start = ((), (), s32[]{:S(2)}) async-start(), calls=%async_computation.11 | async-start | bytes 1114112 | tf_op jit(solution)/shard_map/all_gather | solution.py:9
  312.5 1.4 copy-start.1
  315.7 93.2 %all-gather.31.cloned.1.call-start = ((), (), s32[]{:S(2)}) async-start(), calls=%async_computation.3 | async-start | bytes 2506752 | tf_op jit(solution)/shard_map/all_gather | solution.py:40
  316.1 92.8 %copy-start.2 = (f32[36,128,128]{2,1,0:T(8,128)S(1)}, f32[36,128,128]{2,1,0:T(8,128)}, u32[]{:S(2)}) copy-start(f32[36,128,128]{2,1,0:T(8,128)} %copy-done.1) | copy-start | bytes 7077892
  317.6 136.9 %all-gather.49.cloned.1.call-start = ((), (), s32[]{:S(2)}) async-start(), calls=%async_computation.12 | async-start | bytes 1114112 | tf_op jit(solution)/shard_map/all_gather | solution.py:9
  412.8 1.4 copy-start.3
  416.0 93.0 %all-gather.33.cloned.1.call-start = ((), (), s32[]{:S(2)}) async-start(), calls=%async_computation.4 | async-start | bytes 2506752 | tf_op jit(solution)/shard_map/all_gather | solution.py:40
  416.1 92.9 %copy-start.4 = (f32[36,128,128]{2,1,0:T(8,128)S(1)}, f32[36,128,128]{2,1,0:T(8,128)}, u32[]{:S(2)}) copy-start(f32[36,128,128]{2,1,0:T(8,128)} %copy-done.3) | copy-start | bytes 7077892
  417.6 136.9 %all-gather.51.cloned.1.call-start = ((), (), s32[]{:S(2)}) async-start(), calls=%async_computation.13 | async-start | bytes 1114112 | tf_op jit(solution)/shard_map/all_gather | solution.py:9
  512.9 1.4 copy-start.5
  516.1 93.1 %all-gather.35.cloned.1.call-start = ((), (), s32[]{:S(2)}) async-start(), calls=%async_computation.5 | async-start | bytes 2506752 | tf_op jit(solution)/shard_map/all_gather | solution.py:40
  517.7 136.1 %all-gather.53.cloned.1.call-start = ((), (), s32[]{:S(2)}) async-start(), calls=%async_computation.14 | async-start | bytes 1114112 | tf_op jit(solution)/shard_map/all_gather | solution.py:9
  615.3 93.1 %all-gather.37.cloned.1.call-start = ((), (), s32[]{:S(2)}) async-start(), calls=%async_computation.6 | async-start | bytes 2506752 | tf_op jit(solution)/shard_map/all_gather | solution.py:40
  617.2 136.7 %all-gather.55.cloned.1.call-start = ((), (), s32[]{:S(2)}) async-start(), calls=%async_computation.15 | async-start | bytes 1114112 | tf_op jit(solution)/shard_map/all_gather | solution.py:9
  712.3 1.4 copy-start.7
  715.4 92.5 %all-gather.39.cloned.1.call-start = ((), (), s32[]{:S(2)}) async-start(), calls=%async_computation.7 | async-start | bytes 2506752 | tf_op jit(solution)/shard_map/all_gather | solution.py:40
  721.1 86.8 %copy-start.8 = (f32[36,128,128]{2,1,0:T(8,128)S(1)}, f32[36,128,128]{2,1,0:T(8,128)}, u32[]{:S(2)}) copy-start(f32[36,128,128]{2,1,0:T(8,128)} %copy-done.7) | copy-start | bytes 7077892
Sparse Core Ops, SparseCore 0:
  12.8 41.8 all-gather.40
  57.6 51.6 all-gather.24
  116.5 38.3 all-gather.42
  157.7 51.6 all-gather.26
  215.7 38.3 all-gather.44
  257.0 51.6 all-gather.28
  315.8 38.3 all-gather.46
  357.2 51.6 all-gather.30
  416.1 38.3 all-gather.48
  457.3 51.6 all-gather.32
  516.2 38.3 all-gather.50
  557.4 51.6 all-gather.34
  615.4 38.3 all-gather.52
  656.7 51.6 all-gather.36
  715.6 38.3 all-gather.54
  756.2 51.6 all-gather.38
